TPU v7x, 512 devices: a whole 4x8x8 slice. The times are simulated.
512 devices in a mesh: dp: 2 (over core), ctx: 64 (over z, y), head: 4 (over x).
Axes of the slice: x: 4, y: 8, z: 8, core: 2. Of those that a mesh axis runs over, the one named last changes fastest.
Arguments:
- queries: bfloat16 [2, 8192, 2560], P('dp', 'ctx', 'head'), may hold values from -25 to 25
- keys: bfloat16 [2, 8192, 2560], P('dp', 'ctx', 'head'), may hold values from -25 to 25
- values: bfloat16 [2, 8192, 2560], P('dp', 'ctx', 'head'), may hold values from -6 to 6
- grad_y: bfloat16 [2, 8192, 2560], P('dp', 'ctx', 'head'), may hold values from -6 to 6
- out_gain: float32 [2560], P('head'), may hold values from 0.1 to 1.9
- offsets: int32 [2, 20], P(None, 'head'), may hold values from 0 to 63, as said below
Outputs:
- attended: bfloat16 [2, 8192, 2560], P('dp', 'ctx', 'head')
- query_grad: bfloat16 [2, 8192, 2560], P('dp', 'ctx', 'head')
- key_grad: bfloat16 [2, 8192, 2560], P('dp', 'ctx', 'head')
- value_grad: bfloat16 [2, 8192, 2560], P('dp', 'ctx', 'head')
- gain_grad: float32 [2560], P('head')
Inputs may be any that keep to these rules, and one draw needn't show every extreme that they name: Row 0 holds offsets below 8, row 1 offsets below 64.
All inputs are finite; a program needn't handle non-finite values.
Results may differ from a plain program's by a relative error of at most 0.011.
Values may be sent and summed in bfloat16 or wider, within the bound.
A program may use at most 64 MiB of HBM per device.

v0:
```python
import math
import jax
import jax.numpy as jnp
from jax import lax
from jax.sharding import PartitionSpec as P

HEAD_DIM = 128
SPAN = 4
R1 = 8
EPS = 1e-06


def swapped(block, axis, bit):
    count = lax.axis_size(axis)
    route = []
    for low in range(count):
        high = low | 1 << bit
        if high != low and high < count:
            route += [(low, high), (high, low)]
    return lax.ppermute(block, axis, route)


def pick_rows(source_rows, dilation, shifts):
    row_count, head_count, head_width = source_rows.shape
    grouped = source_rows.reshape(row_count // dilation, dilation, head_count, head_width)
    hit_mask = jnp.arange(dilation, dtype=jnp.int32).reshape(1, dilation, 1, 1) == shifts.reshape(
        1, 1, head_count, 1
    )
    chosen = jnp.where(hit_mask, grouped, jnp.zeros((), source_rows.dtype))
    return jnp.sum(chosen, axis=1, dtype=source_rows.dtype)


def place_rows(row_values, dilation, shifts):
    row_count, head_count, head_width = row_values.shape
    hit_mask = jnp.arange(dilation, dtype=jnp.int32).reshape(1, dilation, 1, 1) == shifts.reshape(
        1, 1, head_count, 1
    )
    spread = jnp.where(hit_mask, row_values[:, None], jnp.zeros((), row_values.dtype))
    return spread.reshape(row_count * dilation, head_count, head_width)


def level_scores(q_rows, k_rows):
    score_scale = 1.0 / math.sqrt(q_rows.shape[-1])
    return (
        jnp.einsum("qhe,khe->hqk", q_rows, k_rows, preferred_element_type=jnp.float32) * score_scale
    )


def attend(q_rows, k_rows, v_rows):
    scores = level_scores(q_rows, k_rows)
    row_max = jnp.max(scores, axis=-1, keepdims=True)
    log_total = row_max[..., 0] + jnp.log(jnp.sum(jnp.exp(scores - row_max), axis=-1))
    soft_rows = jnp.exp(scores - log_total[..., None]).astype(jnp.bfloat16)
    level_out = jnp.einsum("hqk,khe->qhe", soft_rows, v_rows, preferred_element_type=jnp.float32)
    return (level_out, log_total.T)


def score_grads(q_rows, k_rows, v_rows, log_total, grad_low, row_shift):
    score_scale = 1.0 / math.sqrt(q_rows.shape[-1])
    scores = level_scores(q_rows, k_rows)
    exact_soft = jnp.exp(scores - log_total.T[..., None])
    prob_grad = jnp.einsum("qhe,khe->hqk", grad_low, v_rows, preferred_element_type=jnp.float32)
    score_grad = (exact_soft * (prob_grad + row_shift.T[..., None]) * score_scale).astype(
        jnp.bfloat16
    )
    return (score_grad, exact_soft.astype(jnp.bfloat16))


def key_parts(score_grad, soft_low, q_rows, grad_low):
    k_part = jnp.einsum("hqk,qhe->khe", score_grad, q_rows, preferred_element_type=jnp.float32)
    v_part = jnp.einsum("hqk,qhe->khe", soft_low, grad_low, preferred_element_type=jnp.float32)
    return (k_part, v_part)


def query_part(score_grad, k_rows):
    return jnp.einsum("hqk,khe->qhe", score_grad, k_rows, preferred_element_type=jnp.float32)


def shards(queries, keys, values, grad_y, out_gain, offsets):
    tokens = queries.shape[1]
    flat_width = queries.shape[2]
    head_count = flat_width // HEAD_DIM
    row_shape = (tokens, head_count, HEAD_DIM)
    q_own = queries[0].reshape(row_shape)
    k_own = keys[0].reshape(row_shape)
    v_own = values[0].reshape(row_shape)
    ctx_size = lax.axis_size("ctx")
    span_bits = SPAN.bit_length() - 1
    my_place = lax.axis_index("ctx")
    mid_shift = offsets[0]
    top_shift = offsets[1]
    positions = jnp.arange(tokens, dtype=jnp.int32)
    mid_hit = (positions % R1)[:, None] == mid_shift[None, :]
    top_hit = (positions % ctx_size)[:, None] == top_shift[None, :]
    mid_q = pick_rows(q_own, R1, mid_shift)
    mid_k = pick_rows(k_own, R1, mid_shift)
    mid_v = pick_rows(v_own, R1, mid_shift)
    top_q = pick_rows(q_own, ctx_size, top_shift)
    top_k = pick_rows(k_own, ctx_size, top_shift)
    top_v = pick_rows(v_own, ctx_size, top_shift)
    mid_keys = mid_k.reshape(-1, flat_width)
    mid_vals = mid_v.reshape(-1, flat_width)
    top_keys = top_k.reshape(-1, flat_width)
    top_vals = top_v.reshape(-1, flat_width)

    def append_peer(mine, received, level_bit):
        upper_side = my_place >> level_bit & 1 == 1
        return jnp.where(
            upper_side, jnp.concatenate([received, mine], 0), jnp.concatenate([mine, received], 0)
        )

    for level_bit in range(span_bits):
        received = swapped((mid_keys, mid_vals), "ctx", level_bit)
        mid_keys = append_peer(mid_keys, received[0], level_bit)
        mid_vals = append_peer(mid_vals, received[1], level_bit)
    top_keys, top_vals = (
        lax.all_gather(top_keys, "ctx", axis=0, tiled=True),
        lax.all_gather(top_vals, "ctx", axis=0, tiled=True),
    )
    mid_keys = mid_keys.reshape(-1, head_count, HEAD_DIM)
    mid_vals = mid_vals.reshape(-1, head_count, HEAD_DIM)
    top_keys = top_keys.reshape(-1, head_count, HEAD_DIM)
    top_vals = top_vals.reshape(-1, head_count, HEAD_DIM)
    base_out, base_total = attend(q_own, k_own, v_own)
    mid_out, mid_total = attend(mid_q, mid_keys, mid_vals)
    top_out, top_total = attend(top_q, top_keys, top_vals)
    mid_full = place_rows(mid_total[..., None], R1, mid_shift)[..., 0]
    top_full = place_rows(top_total[..., None], ctx_size, top_shift)[..., 0]
    row_max = jnp.maximum(base_total, jnp.where(mid_hit, mid_full, base_total))
    row_max = jnp.maximum(row_max, jnp.where(top_hit, top_full, base_total))
    base_expo = jnp.exp(base_total - row_max)
    mid_expo = jnp.where(mid_hit, jnp.exp(mid_full - row_max), 0.0)
    top_expo = jnp.where(top_hit, jnp.exp(top_full - row_max), 0.0)
    denom = base_expo + mid_expo + top_expo
    base_share = base_expo / denom
    mid_share = mid_expo / denom
    top_share = top_expo / denom
    attn = (
        base_share[..., None] * base_out
        + mid_share[..., None] * place_rows(mid_out, R1, mid_shift)
        + top_share[..., None] * place_rows(top_out, ctx_size, top_shift)
    )
    inv_rms = lax.rsqrt(jnp.mean(attn * attn, axis=-1, keepdims=True) + EPS)
    normed = attn * inv_rms
    gain_rows = out_gain.reshape(head_count, HEAD_DIM)
    attended = (normed * gain_rows).astype(jnp.bfloat16).reshape(1, tokens, flat_width)
    grad_full = grad_y[0].reshape(row_shape).astype(jnp.float32)
    gain_part = jnp.sum(grad_full * normed, axis=0).reshape(flat_width)
    gain_grad = lax.psum(gain_part, ("dp", "ctx"))
    grad_norm = grad_full * gain_rows
    grad_attn = inv_rms * (
        grad_norm - normed * jnp.mean(grad_norm * normed, axis=-1, keepdims=True)
    )
    inner = jnp.sum(grad_attn * attn, axis=-1)
    base_low = (base_share[..., None] * grad_attn).astype(jnp.bfloat16)
    base_shift = -(base_share * inner)
    base_grad, base_soft = score_grads(q_own, k_own, v_own, base_total, base_low, base_shift)
    base_dq = query_part(base_grad, k_own)
    base_dk, base_dv = key_parts(base_grad, base_soft, q_own, base_low)
    mid_sel = pick_rows(mid_share[..., None], R1, mid_shift)[..., 0]
    mid_low = (mid_sel[..., None] * pick_rows(grad_attn, R1, mid_shift)).astype(jnp.bfloat16)
    mid_row_shift = -(mid_sel * pick_rows(inner[..., None], R1, mid_shift)[..., 0])
    mid_grad, mid_soft = score_grads(mid_q, mid_keys, mid_vals, mid_total, mid_low, mid_row_shift)
    mid_dq = query_part(mid_grad, mid_keys)
    mid_dk, mid_dv = key_parts(mid_grad, mid_soft, mid_q, mid_low)
    mid_dk = mid_dk.reshape(-1, flat_width)
    mid_dv = mid_dv.reshape(-1, flat_width)
    for level_bit in reversed(range(span_bits)):
        half_rows = mid_dk.shape[0] // 2
        upper_side = my_place >> level_bit & 1 == 1
        keep_k = jnp.where(upper_side, mid_dk[half_rows:], mid_dk[:half_rows])
        keep_v = jnp.where(upper_side, mid_dv[half_rows:], mid_dv[:half_rows])
        send_k = jnp.where(upper_side, mid_dk[:half_rows], mid_dk[half_rows:])
        send_v = jnp.where(upper_side, mid_dv[:half_rows], mid_dv[half_rows:])
        received = (
            swapped(send_k.astype(jnp.bfloat16), "ctx", level_bit).astype(send_k.dtype),
            swapped(send_v.astype(jnp.bfloat16), "ctx", level_bit).astype(send_v.dtype),
        )
        mid_dk = keep_k + received[0]
        mid_dv = keep_v + received[1]
    mid_dk = mid_dk.reshape(-1, head_count, HEAD_DIM)
    mid_dv = mid_dv.reshape(-1, head_count, HEAD_DIM)
    top_sel = pick_rows(top_share[..., None], ctx_size, top_shift)[..., 0]
    top_low = (top_sel[..., None] * pick_rows(grad_attn, ctx_size, top_shift)).astype(jnp.bfloat16)
    top_row_shift = -(top_sel * pick_rows(inner[..., None], ctx_size, top_shift)[..., 0])
    top_grad, top_soft = score_grads(top_q, top_keys, top_vals, top_total, top_low, top_row_shift)
    top_dq = query_part(top_grad, top_keys)
    gathered_dk, gathered_dv = key_parts(top_grad, top_soft, top_q, top_low)
    summed = (
        lax.psum_scatter(
            gathered_dk.reshape(-1, flat_width), "ctx", scatter_dimension=0, tiled=True
        ),
        lax.psum_scatter(
            gathered_dv.reshape(-1, flat_width), "ctx", scatter_dimension=0, tiled=True
        ),
    )
    top_dk = summed[0].reshape(-1, head_count, HEAD_DIM)
    top_dv = summed[1].reshape(-1, head_count, HEAD_DIM)
    query_grad = (
        base_dq + place_rows(mid_dq, R1, mid_shift) + place_rows(top_dq, ctx_size, top_shift)
    )
    key_grad = base_dk + place_rows(mid_dk, R1, mid_shift) + place_rows(top_dk, ctx_size, top_shift)
    value_grad = (
        base_dv + place_rows(mid_dv, R1, mid_shift) + place_rows(top_dv, ctx_size, top_shift)
    )
    out_shape = (1, tokens, flat_width)
    return (
        attended,
        query_grad.astype(jnp.bfloat16).reshape(out_shape),
        key_grad.astype(jnp.bfloat16).reshape(out_shape),
        value_grad.astype(jnp.bfloat16).reshape(out_shape),
        gain_grad,
    )


def solution(mesh):
    in_specs = (
        P("dp", "ctx", "head"),
        P("dp", "ctx", "head"),
        P("dp", "ctx", "head"),
        P("dp", "ctx", "head"),
        P("head"),
        P(None, "head"),
    )
    out_specs = (
        P("dp", "ctx", "head"),
        P("dp", "ctx", "head"),
        P("dp", "ctx", "head"),
        P("dp", "ctx", "head"),
        P("head"),
    )
    return jax.shard_map(shards, mesh=mesh, in_specs=in_specs, out_specs=out_specs, check_vma=False)
```

profile of v0, /device:TPU:266, one launch (start us, length us, event | category | flops | bytes accessed | tf_op | source)
XLA Modules:
  0.0 443.0 jit_solution(7934693849912801585)
XLA Ops:
  7.2 0.8 slice_bitcast_fusion.1
  8.0 1.5 fusion.26
  9.6 2.4 collective-permute-start
  12.0 3.6 collective-permute-start.2
  16.4 0.7 copy-done.2
  17.8 48.5 %all-gather = bf16[64,2,640]{2,1,0:T(2,128)(2,1)S(1)} all-gather(bf16[1,2,640]{2,1,0:T(2,128)(2,1)S(1)} %reshape.367), channel_id=1, replica_groups=mesh['dp'=2,'ctx'=64,'head'=4] {'ctx'}, dimensions={0}, use_global_device_ids=true | all-gather | bytes 166400 | tf_op jit(solution)/shard_map/all_gather | solution.py:117
  67.0 47.4 %all-gather.1 = bf16[64,2,640]{2,1,0:T(2,128)(2,1)S(1)} all-gather(bf16[1,2,640]{2,1,0:T(2,128)(2,1)S(1)} %reshape.369), channel_id=1, replica_groups=mesh['dp'=2,'ctx'=64,'head'=4] {'ctx'}, dimensions={0}, use_global_device_ids=true | all-gather | bytes 166400 | tf_op jit(solution)/shard_map/all_gather | solution.py:118
  114.6 0.3 fusion.60
  115.4 0.5 copy-done.4
  116.4 1.3 dynamic-slice
  118.4 4.6 %collective-permute-start.1 = (bf16[32,640]{1,0:T(8,128)(2,1)S(1)}, bf16[32,640]{1,0:T(8,128)(2,1)S(1)}, u32[]{:S(2)}, u32[]{:S(2)}) collective-permute-start(bf16[32,640]{1,0:T(8,128)(2,1)S(1)} %maximum_select_fusion.2), channel_id=1, source_target_pairs={{0,8},{8,0},{4,12},{12,4},{16,24},{24,16},{20,28},{28,20},{32,40},... | collective-permute-start | bytes 122888 | tf_op jit(solution)/shard_map/ppermute | solution.py:20
  123.0 2.2 collective-permute-start.3
  126.4 3.4 collective-permute-done.3
  130.0 0.5 multiply_reduce_fusion.3
  130.6 0.7 copy-done.5
  131.2 0.3 multiply_reduce_fusion
  133.0 1.0 fusion.50
  134.1 1.0 fusion.47
  135.1 0.4 fusion.14
  135.6 0.3 convolution_bitcast_fusion.4
  136.1 2.2 collective-permute-start.6
  138.7 4.6 %collective-permute-start.4 = (bf16[32,640]{1,0:T(8,128)(2,1)S(1)}, bf16[32,640]{1,0:T(8,128)(2,1)S(1)}, u32[]{:S(2)}, u32[]{:S(2)}) collective-permute-start(bf16[32,640]{1,0:T(8,128)(2,1)S(1)} %copy_bitcast_fusion.1), channel_id=1, source_target_pairs={{0,8},{8,0},{4,12},{12,4},{16,24},{24,16},{20,28},{28,20},{32,40},... | collective-permute-start | bytes 122888 | tf_op jit(solution)/shard_map/ppermute | solution.py:20
  143.4 0.8 copy.198
  144.3 275.7 %psum.7 = f32[640]{0:T(1024)} all-reduce(f32[640]{0:T(1024)S(1)} %bitcast.253), channel_id=1, replica_groups=mesh['dp'=2,'ctx'=64,'head'=4] {'dp','ctx'}, use_global_device_ids=true, to_apply=%region_24.25 | all-reduce | flops 640 | bytes 5120 | tf_op jit(solution)/shard_map/psum | solution.py:149
  420.0 4.7 %collective-permute-start.7 = (bf16[16,640]{1,0:T(8,128)(2,1)S(1)}, bf16[16,640]{1,0:T(8,128)(2,1)S(1)}, u32[]{:S(2)}, u32[]{:S(2)}) collective-permute-start(bf16[16,640]{1,0:T(8,128)(2,1)S(1)} %select_convert_fusion.2), channel_id=1, source_target_pairs={{0,4},{4,0},{8,12},{12,8},{16,20},{20,16},{24,28},{28,24},{32,36},... | collective-permute-start | bytes 61448 | tf_op jit(solution)/shard_map/ppermute | solution.py:20
  424.8 1.9 collective-permute-start.5
  426.8 3.7 collective-permute-done.5
  430.6 1.2 constant_dynamic-slice_fusion.1
  432.8 0.8 copy.200
  434.1 0.8 copy.199
  434.9 0.3 fusion.13
  435.4 0.8 copy.201
  (105 shorter events, 9.0 us)
Async XLA Ops:
  7.2 423.4 %all-reduce.5.cloned.1.call-start = ((), (), s32[]{:S(2)}) async-start(), calls=%async_computation | async-start | bytes 1310720
  8.0 7.6 %copy-start = (bf16[1,128,640]{2,1,0:T(8,128)(2,1)S(1)}, bf16[1,128,640]{2,1,0:T(8,128)(2,1)}, u32[]{:S(2)}) copy-start(bf16[1,128,640]{2,1,0:T(8,128)(2,1)} %param.6) | copy-start | bytes 491524
  9.6 108.7 %collective-permute-start = (bf16[16,640]{1,0:T(8,128)(2,1)S(1)}, bf16[16,640]{1,0:T(8,128)(2,1)S(1)}, u32[]{:S(2)}, u32[]{:S(2)}) collective-permute-start(bf16[16,640]{1,0:T(8,128)(2,1)S(1)} %copy_bitcast_fusion.7), channel_id=1, source_target_pairs={{0,4},{4,0},{8,12},{12,8},{16,20},{20,16},{24,28},{28,24},{32,36},... | collective-permute-start | bytes 61448 | tf_op jit(solution)/shard_map/ppermute | solution.py:20
  12.0 3.8 copy-start.1
  12.0 106.4 %collective-permute-start.2 = (bf16[16,640]{1,0:T(8,128)(2,1)S(1)}, bf16[16,640]{1,0:T(8,128)(2,1)S(1)}, u32[]{:S(2)}, u32[]{:S(2)}) collective-permute-start(bf16[16,640]{1,0:T(8,128)(2,1)S(1)} %copy_bitcast_fusion.6), channel_id=1, source_target_pairs={{0,4},{4,0},{8,12},{12,8},{16,20},{20,16},{24,28},{28,24},{32,36},... | collective-permute-start | bytes 61448 | tf_op jit(solution)/shard_map/ppermute | solution.py:20
  16.2 0.9 copy-start.2
  115.0 0.9 copy-start.4
  118.4 6.9 %collective-permute-start.1 = (bf16[32,640]{1,0:T(8,128)(2,1)S(1)}, bf16[32,640]{1,0:T(8,128)(2,1)S(1)}, u32[]{:S(2)}, u32[]{:S(2)}) collective-permute-start(bf16[32,640]{1,0:T(8,128)(2,1)S(1)} %maximum_select_fusion.2), channel_id=1, source_target_pairs={{0,8},{8,0},{4,12},{12,4},{16,24},{24,16},{20,28},{28,20},{32,40},... | collective-permute-start | bytes 122888 | tf_op jit(solution)/shard_map/ppermute | solution.py:20
  123.0 6.8 %collective-permute-start.3 = (bf16[32,640]{1,0:T(8,128)(2,1)S(1)}, bf16[32,640]{1,0:T(8,128)(2,1)S(1)}, u32[]{:S(2)}, u32[]{:S(2)}) collective-permute-start(bf16[32,640]{1,0:T(8,128)(2,1)S(1)} %maximum_select_fusion.4), channel_id=1, source_target_pairs={{0,8},{8,0},{4,12},{12,4},{16,24},{24,16},{20,28},{28,20},{32,40},... | collective-permute-start | bytes 122888 | tf_op jit(solution)/shard_map/ppermute | solution.py:20
  130.5 0.7 copy-start.5
  136.1 283.9 %collective-permute-start.6 = (bf16[32,640]{1,0:T(8,128)(2,1)S(1)}, bf16[32,640]{1,0:T(8,128)(2,1)S(1)}, u32[]{:S(2)}, u32[]{:S(2)}) collective-permute-start(bf16[32,640]{1,0:T(8,128)(2,1)S(1)} %copy_bitcast_fusion), channel_id=1, source_target_pairs={{0,8},{8,0},{4,12},{12,4},{16,24},{24,16},{20,28},{28,20},{32,40},... | collective-permute-start | bytes 122888 | tf_op jit(solution)/shard_map/ppermute | solution.py:20
  138.7 286.1 %collective-permute-start.4 = (bf16[32,640]{1,0:T(8,128)(2,1)S(1)}, bf16[32,640]{1,0:T(8,128)(2,1)S(1)}, u32[]{:S(2)}, u32[]{:S(2)}) collective-permute-start(bf16[32,640]{1,0:T(8,128)(2,1)S(1)} %copy_bitcast_fusion.1), channel_id=1, source_target_pairs={{0,8},{8,0},{4,12},{12,4},{16,24},{24,16},{20,28},{28,20},{32,40},... | collective-permute-start | bytes 122888 | tf_op jit(solution)/shard_map/ppermute | solution.py:20
  420.0 6.7 %collective-permute-start.7 = (bf16[16,640]{1,0:T(8,128)(2,1)S(1)}, bf16[16,640]{1,0:T(8,128)(2,1)S(1)}, u32[]{:S(2)}, u32[]{:S(2)}) collective-permute-start(bf16[16,640]{1,0:T(8,128)(2,1)S(1)} %select_convert_fusion.2), channel_id=1, source_target_pairs={{0,4},{4,0},{8,12},{12,8},{16,20},{20,16},{24,28},{28,24},{32,36},... | collective-permute-start | bytes 61448 | tf_op jit(solution)/shard_map/ppermute | solution.py:20
  424.8 5.7 %collective-permute-start.5 = (bf16[16,640]{1,0:T(8,128)(2,1)S(1)}, bf16[16,640]{1,0:T(8,128)(2,1)S(1)}, u32[]{:S(2)}, u32[]{:S(2)}) collective-permute-start(bf16[16,640]{1,0:T(8,128)(2,1)S(1)} %select_convert_fusion.3), channel_id=1, source_target_pairs={{0,4},{4,0},{8,12},{12,8},{16,20},{20,16},{24,28},{28,24},{32,36},... | collective-permute-start | bytes 61448 | tf_op jit(solution)/shard_map/ppermute | solution.py:20
  430.6 1.2 copy-start.3
Sparse Core Ops, SparseCore 0:
  144.4 154.0 all-reduce.4
where the time goes:
time: 444 us; the launch traced here: 443 us
  blocking collectives  372 us (84%)
  starting transfers between devices  26.2 us (6%)
  between operations  15.2 us (3%)
  local copies, waits for them, and re-layouts  12.3 us (3%)
  waiting for transfers between devices  7.26 us (2%)
  matrix products  6.13 us (1%)
    psum x1, blocking collectives, shards(): gain_grad = lax.psum(gain_part, ('dp', 'ctx'))  276 us
    all_gather x1, blocking collectives, shards(): lax.all_gather(top_keys, 'ctx', axis=0, tiled=True)  48.5 us
    all_gather x1, blocking collectives, shards(): lax.all_gather(top_vals, 'ctx', axis=0, tiled=True)  47.4 us
    ppermute x8, starting transfers between devices, swapped(): return lax.ppermute(block, axis, route)  26.1 us
  transfers between devices with their start and end apart: 9, of which 3 were waited for; matrix products, arithmetic and copies ran while one was open for 2% of the time, Pallas kernels for 0%

commit v1 on v0

--- a/solution.py
+++ b/solution.py
@@ -146,7 +146,8 @@
     attended = (normed * gain_rows).astype(jnp.bfloat16).reshape(1, tokens, flat_width)
     grad_full = grad_y[0].reshape(row_shape).astype(jnp.float32)
     gain_part = jnp.sum(grad_full * normed, axis=0).reshape(flat_width)
-    gain_grad = lax.psum(gain_part, ("dp", "ctx"))
+    one_axis = lax.psum(gain_part, "ctx")
+    gain_grad = lax.psum(one_axis, "dp")
     grad_norm = grad_full * gain_rows
     grad_attn = inv_rms * (
         grad_norm - normed * jnp.mean(grad_norm * normed, axis=-1, keepdims=True)

time: 444 us -> 317 us (0.71)
  the two profiles are of different devices: /device:TPU:266 before, /device:TPU:2 now
where the time goes in v1:
time: 317 us
  blocking collectives  248 us (78%)
  starting transfers between devices  25.3 us (8%)
  between operations  15.2 us (5%)
  local copies, waits for them, and re-layouts  12.3 us (4%)
  matrix products  6.13 us (2%)
  waiting for transfers between devices  5.29 us (2%)
  other arithmetic  4.4 us (1%)
    psum x1, blocking collectives, shards(): one_axis = lax.psum(gain_part, 'ctx')  141 us
    all_gather x1, blocking collectives, shards(): lax.all_gather(top_keys, 'ctx', axis=0, tiled=True)  56.5 us
    all_gather x1, blocking collectives, shards(): lax.all_gather(top_vals, 'ctx', axis=0, tiled=True)  47.7 us
    ppermute x8, starting transfers between devices, swapped(): return lax.ppermute(block, axis, route)  25.3 us
    unnamed x25, local copies, waits for them, and re-layouts  8.48 us
  transfers between devices with their start and end apart: 9, of which 4 were waited for; matrix products, arithmetic and copies ran while one was open for 2% of the time, Pallas kernels for 0%

profile of v1, /device:TPU:2, one launch (start us, length us, event | category | flops | bytes accessed | tf_op | source)
XLA Modules:
  0.0 316.6 jit_solution(4417123547839130465)
XLA Ops:
  7.2 0.8 slice_bitcast_fusion.1
  8.0 1.5 fusion.26
  9.6 3.5 %collective-permute-start = (bf16[16,640]{1,0:T(8,128)(2,1)S(1)}, bf16[16,640]{1,0:T(8,128)(2,1)S(1)}, u32[]{:S(2)}, u32[]{:S(2)}) collective-permute-start(bf16[16,640]{1,0:T(8,128)(2,1)S(1)} %copy_bitcast_fusion.7), channel_id=1, source_target_pairs={{0,4},{4,0},{8,12},{12,8},{16,20},{20,16},{24,28},{28,24},{32,36},... | collective-permute-start | bytes 61448 | tf_op jit(solution)/shard_map/ppermute | solution.py:20
  13.1 2.5 collective-permute-start.2
  16.4 0.7 copy-done.2
  17.8 56.5 %all-gather = bf16[64,2,640]{2,1,0:T(2,128)(2,1)S(1)} all-gather(bf16[1,2,640]{2,1,0:T(2,128)(2,1)S(1)} %reshape.367), channel_id=1, replica_groups=mesh['dp'=2,'ctx'=64,'head'=4] {'ctx'}, dimensions={0}, use_global_device_ids=true | all-gather | bytes 166400 | tf_op jit(solution)/shard_map/all_gather | solution.py:117
  75.0 47.7 %all-gather.1 = bf16[64,2,640]{2,1,0:T(2,128)(2,1)S(1)} all-gather(bf16[1,2,640]{2,1,0:T(2,128)(2,1)S(1)} %reshape.369), channel_id=1, replica_groups=mesh['dp'=2,'ctx'=64,'head'=4] {'ctx'}, dimensions={0}, use_global_device_ids=true | all-gather | bytes 166400 | tf_op jit(solution)/shard_map/all_gather | solution.py:118
  123.7 0.5 copy-done.4
  124.7 1.3 dynamic-slice
  126.7 2.7 collective-permute-start.1
  129.5 4.0 %collective-permute-start.3 = (bf16[32,640]{1,0:T(8,128)(2,1)S(1)}, bf16[32,640]{1,0:T(8,128)(2,1)S(1)}, u32[]{:S(2)}, u32[]{:S(2)}) collective-permute-start(bf16[32,640]{1,0:T(8,128)(2,1)S(1)} %maximum_select_fusion.4), channel_id=1, source_target_pairs={{0,8},{8,0},{4,12},{12,4},{16,24},{24,16},{20,28},{28,20},{32,40},... | collective-permute-start | bytes 122888 | tf_op jit(solution)/shard_map/ppermute | solution.py:20
  133.5 0.5 collective-permute-done.1
  135.1 1.2 collective-permute-done.3
  136.5 0.5 multiply_reduce_fusion.3
  137.0 0.7 copy-done.5
  139.5 1.0 fusion.50
  140.5 1.0 fusion.47
  141.5 0.4 fusion.14
  142.0 0.3 convolution_bitcast_fusion.4
  142.6 4.0 %collective-permute-start.6 = (bf16[32,640]{1,0:T(8,128)(2,1)S(1)}, bf16[32,640]{1,0:T(8,128)(2,1)S(1)}, u32[]{:S(2)}, u32[]{:S(2)}) collective-permute-start(bf16[32,640]{1,0:T(8,128)(2,1)S(1)} %copy_bitcast_fusion), channel_id=1, source_target_pairs={{0,8},{8,0},{4,12},{12,4},{16,24},{24,16},{20,28},{28,20},{32,40},... | collective-permute-start | bytes 122888 | tf_op jit(solution)/shard_map/ppermute | solution.py:20
  147.0 2.7 collective-permute-start.4
  149.9 0.8 copy.198
  150.8 140.8 %psum.14 = f32[640]{0:T(1024)S(1)} all-reduce(f32[640]{0:T(1024)S(1)} %bitcast.253), channel_id=1, replica_groups=mesh['dp'=2,'ctx'=64,'head'=4] {'ctx'}, use_global_device_ids=true, to_apply=%region_24.25 | all-reduce | flops 640 | bytes 5120 | tf_op jit(solution)/shard_map/psum | solution.py:149
  291.5 3.0 psum.15
  294.6 1.9 collective-permute-start.7
  296.6 3.9 %collective-permute-start.5 = (bf16[16,640]{1,0:T(8,128)(2,1)S(1)}, bf16[16,640]{1,0:T(8,128)(2,1)S(1)}, u32[]{:S(2)}, u32[]{:S(2)}) collective-permute-start(bf16[16,640]{1,0:T(8,128)(2,1)S(1)} %select_convert_fusion.3), channel_id=1, source_target_pairs={{0,4},{4,0},{8,12},{12,8},{16,20},{20,16},{24,28},{28,24},{32,36},... | collective-permute-start | bytes 61448 | tf_op jit(solution)/shard_map/ppermute | solution.py:20
  300.6 1.8 collective-permute-done.5
  302.3 1.8 all-reduce.5.cloned.1.call-done
  304.2 1.2 constant_dynamic-slice_fusion.1
  306.4 0.8 copy.200
  307.7 0.8 copy.199
  309.0 0.8 copy.201
  (106 shorter events, 9.8 us)
Async XLA Ops:
  7.2 297.0 %all-reduce.5.cloned.1.call-start = ((), (), s32[]{:S(2)}) async-start(), calls=%async_computation | async-start | bytes 1310720
  8.0 7.6 %copy-start = (bf16[1,128,640]{2,1,0:T(8,128)(2,1)S(1)}, bf16[1,128,640]{2,1,0:T(8,128)(2,1)}, u32[]{:S(2)}) copy-start(bf16[1,128,640]{2,1,0:T(8,128)(2,1)} %param.6) | copy-start | bytes 491524
  9.6 117.0 %collective-permute-start = (bf16[16,640]{1,0:T(8,128)(2,1)S(1)}, bf16[16,640]{1,0:T(8,128)(2,1)S(1)}, u32[]{:S(2)}, u32[]{:S(2)}) collective-permute-start(bf16[16,640]{1,0:T(8,128)(2,1)S(1)} %copy_bitcast_fusion.7), channel_id=1, source_target_pairs={{0,4},{4,0},{8,12},{12,8},{16,20},{20,16},{24,28},{28,24},{32,36},... | collective-permute-start | bytes 61448 | tf_op jit(solution)/shard_map/ppermute | solution.py:20
  13.1 2.7 copy-start.1
  13.1 113.6 %collective-permute-start.2 = (bf16[16,640]{1,0:T(8,128)(2,1)S(1)}, bf16[16,640]{1,0:T(8,128)(2,1)S(1)}, u32[]{:S(2)}, u32[]{:S(2)}) collective-permute-start(bf16[16,640]{1,0:T(8,128)(2,1)S(1)} %copy_bitcast_fusion.6), channel_id=1, source_target_pairs={{0,4},{4,0},{8,12},{12,8},{16,20},{20,16},{24,28},{28,24},{32,36},... | collective-permute-start | bytes 61448 | tf_op jit(solution)/shard_map/ppermute | solution.py:20
  16.2 0.9 copy-start.2
  123.3 0.9 copy-start.4
  126.7 7.2 %collective-permute-start.1 = (bf16[32,640]{1,0:T(8,128)(2,1)S(1)}, bf16[32,640]{1,0:T(8,128)(2,1)S(1)}, u32[]{:S(2)}, u32[]{:S(2)}) collective-permute-start(bf16[32,640]{1,0:T(8,128)(2,1)S(1)} %maximum_select_fusion.2), channel_id=1, source_target_pairs={{0,8},{8,0},{4,12},{12,4},{16,24},{24,16},{20,28},{28,20},{32,40},... | collective-permute-start | bytes 122888 | tf_op jit(solution)/shard_map/ppermute | solution.py:20
  129.5 6.8 %collective-permute-start.3 = (bf16[32,640]{1,0:T(8,128)(2,1)S(1)}, bf16[32,640]{1,0:T(8,128)(2,1)S(1)}, u32[]{:S(2)}, u32[]{:S(2)}) collective-permute-start(bf16[32,640]{1,0:T(8,128)(2,1)S(1)} %maximum_select_fusion.4), channel_id=1, source_target_pairs={{0,8},{8,0},{4,12},{12,4},{16,24},{24,16},{20,28},{28,20},{32,40},... | collective-permute-start | bytes 122888 | tf_op jit(solution)/shard_map/ppermute | solution.py:20
  137.0 0.7 copy-start.5
  142.6 152.0 %collective-permute-start.6 = (bf16[32,640]{1,0:T(8,128)(2,1)S(1)}, bf16[32,640]{1,0:T(8,128)(2,1)S(1)}, u32[]{:S(2)}, u32[]{:S(2)}) collective-permute-start(bf16[32,640]{1,0:T(8,128)(2,1)S(1)} %copy_bitcast_fusion), channel_id=1, source_target_pairs={{0,8},{8,0},{4,12},{12,4},{16,24},{24,16},{20,28},{28,20},{32,40},... | collective-permute-start | bytes 122888 | tf_op jit(solution)/shard_map/ppermute | solution.py:20
  147.0 149.5 %collective-permute-start.4 = (bf16[32,640]{1,0:T(8,128)(2,1)S(1)}, bf16[32,640]{1,0:T(8,128)(2,1)S(1)}, u32[]{:S(2)}, u32[]{:S(2)}) collective-permute-start(bf16[32,640]{1,0:T(8,128)(2,1)S(1)} %copy_bitcast_fusion.1), channel_id=1, source_target_pairs={{0,8},{8,0},{4,12},{12,4},{16,24},{24,16},{20,28},{28,20},{32,40},... | collective-permute-start | bytes 122888 | tf_op jit(solution)/shard_map/ppermute | solution.py:20
  294.6 5.9 %collective-permute-start.7 = (bf16[16,640]{1,0:T(8,128)(2,1)S(1)}, bf16[16,640]{1,0:T(8,128)(2,1)S(1)}, u32[]{:S(2)}, u32[]{:S(2)}) collective-permute-start(bf16[16,640]{1,0:T(8,128)(2,1)S(1)} %select_convert_fusion.2), channel_id=1, source_target_pairs={{0,4},{4,0},{8,12},{12,8},{16,20},{20,16},{24,28},{28,24},{32,36},... | collective-permute-start | bytes 61448 | tf_op jit(solution)/shard_map/ppermute | solution.py:20
  296.6 5.7 %collective-permute-start.5 = (bf16[16,640]{1,0:T(8,128)(2,1)S(1)}, bf16[16,640]{1,0:T(8,128)(2,1)S(1)}, u32[]{:S(2)}, u32[]{:S(2)}) collective-permute-start(bf16[16,640]{1,0:T(8,128)(2,1)S(1)} %select_convert_fusion.3), channel_id=1, source_target_pairs={{0,4},{4,0},{8,12},{12,8},{16,20},{20,16},{24,28},{28,24},{32,36},... | collective-permute-start | bytes 61448 | tf_op jit(solution)/shard_map/ppermute | solution.py:20
  304.2 1.2 copy-start.3
Sparse Core Ops, SparseCore 0:
  150.9 153.2 all-reduce.4
